TPU v7x, 32 devices: a whole 2x2x4 slice. The times are simulated.
32 devices in a mesh: groups: 2 (over x), vel: 16 (over z, y, core).
Axes of the slice: x: 2, y: 2, z: 4, core: 2. Of those that a mesh axis runs over, the one named last changes fastest.
Arguments:
- signal: bfloat16 [32, 8, 512], P(('groups', 'vel')), parts along dimension 0, may hold values from -6 to 6
- weight: bfloat16 [32, 8, 512], P(('groups', 'vel')), parts along dimension 0, may hold values from 0.25 to 4
- shifts: int32 [16, 16, 2], P('vel'), may hold values from -15 to 15, as said below
- phases: int32 [16, 16, 2], P('vel'), may hold values from 0 to 7, as said below
Outputs:
- likelihood: float32 [32, 8, 512], P(('groups', 'vel')), parts along dimension 0
- best_likelihood: float32 [16, 512], P('groups'), parts along dimension 0
There are 2 independent parts, one for each index of `groups`. A program takes and returns all parts, laid end to end along the dimension named above; an argument that names none is the same for every part. Nothing has to cross between parts.
Inputs may be any that keep to these rules, and one draw needn't show every extreme that they name: shifts[v, e] = floor(o / 8) of offsets o in eighths of a pixel that grow with the exposure index e for each velocity: column offset a_v e with a_v in -8..8, row offset floor(b_v e / 16) with b_v in -8..8; some velocity has a_v = 8 and another a_v = -8. phases[v, e] = the same offsets modulo 8.
All inputs are finite; a program needn't handle non-finite values.
Results may differ from a plain program's by a relative error of at most 0.0003.
Values may be sent and summed in bfloat16 or wider, within the bound.
A program may use at most 64 MiB of HBM per device.

v0:
```python
import jax
import jax.numpy as jnp
from jax import lax
from jax.sharding import PartitionSpec as P


def tap_table():
    fraction = jnp.arange(8, dtype=jnp.float32) / 8.0
    position = (jnp.arange(6, dtype=jnp.int32) - 2).astype(jnp.float32)
    distance = position[None, :] - fraction[:, None]
    raw_taps = jnp.sinc(distance) * jnp.sinc(distance / 3.0)
    return (raw_taps / jnp.sum(raw_taps, axis=1, keepdims=True)).astype(jnp.float32)


def pick_taps(coefficients, phase_index):
    choose = (jnp.arange(coefficients.shape[0], dtype=jnp.int32) == phase_index).astype(jnp.float32)
    return jnp.sum(choose[:, None] * coefficients, axis=0)


def place_pair(padded, shift_pair, phase_pair, coefficients, margin, columns, reach):
    height = padded.shape[1]
    col_taps = pick_taps(coefficients, phase_pair[1])
    row_taps = pick_taps(coefficients, phase_pair[0])
    anchor = shift_pair[0] * 0
    col_start = reach + shift_pair[1] - 2
    slab = lax.dynamic_slice(padded, (anchor, anchor, col_start), (2, height, columns + 5)).astype(
        jnp.float32
    )
    row_pass = sum(
        (
            col_taps[tap_index] * slab[:, :, tap_index : tap_index + columns]
            for tap_index in range(6)
        )
    )
    tall = jnp.pad(row_pass, ((0, 0), (margin, margin), (0, 0)))
    row_start = margin + shift_pair[0] - 2
    slab_rows = lax.dynamic_slice(tall, (anchor, row_start, anchor), (2, height + 5, columns))
    return sum(
        (
            row_taps[tap_index] * slab_rows[:, tap_index : tap_index + height, :]
            for tap_index in range(6)
        )
    )


def place_block(padded, shift_block, phase_block, coefficients, margin, columns, reach):
    placed = jax.vmap(
        lambda image, shift_pair, phase_pair: place_pair(
            image, shift_pair, phase_pair, coefficients, margin, columns, reach
        )
    )(padded, shift_block, phase_block)
    return jnp.sum(placed, axis=0)


def stack_velocities(padded, shift_rows, phase_rows, coefficients, margin, columns, reach):
    count = padded.shape[0]
    height = padded.shape[2]
    block = 32 if count % 32 == 0 else count
    groups_count = count // block

    def one_velocity(inputs):
        shift_set, phase_set = inputs
        if groups_count == 1:
            return place_block(padded, shift_set, phase_set, coefficients, margin, columns, reach)
        blocked = padded.reshape((groups_count, block) + padded.shape[1:])
        shift_blocks = shift_set.reshape((groups_count, block, 2))
        phase_blocks = phase_set.reshape((groups_count, block, 2))

        def add_block(total, item):
            images, shift_block, phase_block = item
            return (
                total
                + place_block(
                    images, shift_block, phase_block, coefficients, margin, columns, reach
                ),
                None,
            )

        start = jnp.zeros((2, height, columns), jnp.float32)
        total, unused = lax.scan(add_block, start, (blocked, shift_blocks, phase_blocks))
        return total

    return lax.map(one_velocity, (shift_rows, phase_rows))


def widen(signal_part, weight_part, reach):
    images = jnp.stack([signal_part, weight_part], axis=1)
    return jnp.pad(images, ((0, 0), (0, 0), (0, 0), (reach, reach)))


def body(signal, weight, shifts, phases):
    coefficients = tap_table()
    columns = signal.shape[2]
    margin = shifts.shape[1] // 16 + 6
    reach = shifts.shape[1] + 3
    gathered_signal, gathered_weight = (
        lax.all_gather(signal, "vel", axis=0, tiled=True),
        lax.all_gather(weight, "vel", axis=0, tiled=True),
    )
    summed = stack_velocities(
        widen(gathered_signal, gathered_weight, reach),
        shifts,
        phases,
        coefficients,
        margin,
        columns,
        reach,
    )
    likelihood = summed[:, 0] / jnp.sqrt(jnp.maximum(summed[:, 1], 1.0))
    best_likelihood = lax.pmax(jnp.max(likelihood, axis=0), "vel")
    return (likelihood, best_likelihood)


def solution(mesh):
    in_specs = (
        P(("groups", "vel"), None, None),
        P(("groups", "vel"), None, None),
        P("vel", None, None),
        P("vel", None, None),
    )
    out_specs = (P(("groups", "vel"), None, None), P("groups", None))
    return jax.shard_map(body, mesh=mesh, in_specs=in_specs, out_specs=out_specs, check_vma=False)
```

profile of v0, /device:TPU:0, one launch (start us, length us, event | category | flops | bytes accessed | tf_op | source)
XLA Modules:
  0.0 174.9 jit_solution(8193985154500921316)
XLA Ops:
  0.6 23.7 %all_gather.7 = bf16[16,8,512]{2,1,0:T(8,128)(2,1)S(1)} all-gather(bf16[1,8,512]{2,1,0:T(8,128)(2,1)} %param.6), channel_id=1, replica_groups=mesh['groups'=2,'vel'=16] {'vel'}, dimensions={0}, use_global_device_ids=true | all-gather | bytes 139264 | tf_op jit(solution)/shard_map/all_gather | solution.py:98
  24.3 7.5 %copy.24 = bf16[16,1,8,512]{2,1,0,3:T(2,128)(2,1)} copy(bf16[16,1,8,512]{3,2,0,1:T(8,128)(2,1)S(1)} %bitcast.42) | data formatting | bytes 262144 | tf_op jit(solution)/shard_map/stack | solution.py:87
  31.9 18.0 %all_gather.6 = bf16[16,8,512]{2,1,0:T(8,128)(2,1)S(1)} all-gather(bf16[1,8,512]{2,1,0:T(8,128)(2,1)} %param.5), channel_id=1, replica_groups=mesh['groups'=2,'vel'=16] {'vel'}, dimensions={0}, use_global_device_ids=true | all-gather | bytes 139264 | tf_op jit(solution)/shard_map/all_gather | solution.py:97
  49.9 7.5 %copy.23 = bf16[16,1,8,512]{2,1,0,3:T(2,128)(2,1)} copy(bf16[16,1,8,512]{3,2,0,1:T(8,128)(2,1)S(1)} %bitcast.43) | data formatting | bytes 262144 | tf_op jit(solution)/shard_map/stack | solution.py:87
  57.4 0.0 copy-start
  57.4 28.2 %select_maximum_fusion = bf16[16,2,8,550]{2,1,0,3:T(2,128)(2,1)} fusion(bf16[16,1,8,512]{2,1,0,3:T(2,128)(2,1)} %copy.24, bf16[16,1,8,512]{2,1,0,3:T(2,128)(2,1)} %copy.23), kind=kLoop, calls=%fused_computation.3 | loop fusion | flops 1267200 | bytes 543744 | tf_op jit(solution)/shard_map/stack | solution.py:87
  85.6 0.0 copy-start.1
  85.6 0.0 copy-done
  85.6 15.2 %gather_fusion = bf16[16,2,8,517]{2,1,3,0:T(2,128)(2,1)} fusion(bf16[16,2,8,550]{2,1,0,3:T(2,128)(2,1)} %select_maximum_fusion, s32[16]{0:T(128)S(1)} %get-tuple-element.42), kind=kCustom, calls=%fused_computation | custom fusion | bytes 529664 | tf_op jit(solution)/shard_map/while/body/eval_jaxpr/vmap()/gather | solution.py:26
  100.8 9.2 %copy.25 = bf16[16,2,8,517]{3,2,1,0:T(8,128)(2,1)S(1)} copy(bf16[16,2,8,517]{2,1,3,0:T(2,128)(2,1)} %gather_fusion) | data formatting | bytes 529408 | tf_op jit(solution)/shard_map/while/body/eval_jaxpr/vmap()/gather | solution.py:26
  110.0 0.1 convert_element_type.40
  110.1 0.2 fusion.58
  110.3 0.1 broadcast_divide_fusion
  110.4 0.1 copy.22
  110.5 0.0 copy-done.1
  110.5 0.1 multiply_reduce_fusion.1
  110.6 0.9 fusion.5
  111.5 0.4 copy.29
  111.9 0.5 pad.11.clone
  112.4 1.5 gather_fusion.1
  113.9 1.2 fusion.10
  115.2 0.6 copy.27
  115.8 59.1 %pmax.7 = f32[8,512]{1,0:T(8,128)} all-reduce(f32[8,512]{1,0:T(8,128)S(1)} %bitcast.46), channel_id=1, replica_groups=mesh['groups'=2,'vel'=16] {'vel'}, use_global_device_ids=true, to_apply=%region_4.6 | all-reduce | flops 4096 | bytes 32768 | tf_op jit(solution)/shard_map/pmax | solution.py:110
  (10 shorter events, 0.1 us)
Async XLA Ops:
  57.4 28.2 %copy-start = (s32[1,16,2]{1,2,0:T(2,128)S(1)}, s32[1,16,2]{1,2,0:T(2,128)}, u32[]{:S(2)}) copy-start(s32[1,16,2]{1,2,0:T(2,128)} %param.7) | copy-start | bytes 388
  85.6 24.9 %copy-start.1 = (s32[1,16,2]{1,2,0:T(2,128)S(1)}, s32[1,16,2]{1,2,0:T(2,128)}, u32[]{:S(2)}) copy-start(s32[1,16,2]{1,2,0:T(2,128)} %param.8) | copy-start | bytes 388
where the time goes:
time: 175 us
  blocking collectives  101 us (58%)
  local copies, waits for them, and re-layouts  42.5 us (24%)
  other arithmetic  30.8 us (18%)
    pmax x1, blocking collectives, body(): best_likelihood = lax.pmax(jnp.max(likelihood, axis=0), 'vel')  59.1 us
    another operation x1, other arithmetic, widen(): images = jnp.stack([signal_part, weight_part], axis=1)  28.2 us
    gather x2, local copies, waits for them, and re-layouts, place_pair(): lax.dynamic_slice(padded, (anchor, anchor, col_start), (2, height, column...  24.4 us
    all_gather x1, blocking collectives, body(): lax.all_gather(weight, 'vel', axis=0, tiled=True)  23.7 us
    all_gather x1, blocking collectives, body(): lax.all_gather(signal, 'vel', axis=0, tiled=True)  18 us
    another operation x2, local copies, waits for them, and re-layouts, widen(): images = jnp.stack([signal_part, weight_part], axis=1)  15 us

commit v1 on v0

--- a/solution.py
+++ b/solution.py
@@ -2,6 +2,28 @@
 import jax.numpy as jnp
 from jax import lax
 from jax.sharding import PartitionSpec as P
+
+
+def joined_along(blocks, dim):
+    blocks = jnp.moveaxis(blocks, 0, dim)
+    dims = blocks.shape
+    return blocks.reshape(*dims[:dim], dims[dim] * dims[dim + 1], *dims[dim + 2 :])
+
+
+def gather_around(array, axis, dim):
+    size = lax.axis_size(axis)
+    pairs = [(i, (i + 1) % size) for i in range(size)]
+    back = [(b, a) for a, b in pairs]
+    lower, upper = ([], [])
+    for lap in range(size - 1):
+        if lap % 2 == 0:
+            lower.append(lax.ppermute(lower[-1] if lower else array, axis, pairs))
+        else:
+            upper.append(lax.ppermute(upper[-1] if upper else array, axis, back))
+    blocks = jnp.stack([*lower[::-1], array, *upper])
+    shift = lax.axis_index(axis) - len(lower)
+    blocks = blocks[(jnp.arange(size) - shift) % size]
+    return joined_along(blocks, dim)
 
 
 def tap_table():
@@ -94,7 +116,7 @@
     margin = shifts.shape[1] // 16 + 6
     reach = shifts.shape[1] + 3
     gathered_signal, gathered_weight = (
-        lax.all_gather(signal, "vel", axis=0, tiled=True),
+        gather_around(signal, "vel", 0),
         lax.all_gather(weight, "vel", axis=0, tiled=True),
     )
     summed = stack_velocities(

time: 175 us -> 199 us (1.14)
  starting transfers between devices: 0 us -> 28.9 us
  blocking collectives: 101 us -> 80.5 us
  waiting for transfers between devices: 0 us -> 13.1 us
    ppermute x0 -> x15, starting transfers between devices: none -> 28.9 us  [the longest x7 28.4 us: gather_around(): upper.append(lax.ppermute(upper[-1] if upper else array, axis, back))]
    all_gather x1 -> x0, blocking collectives: 18 us -> none  [body(): lax.all_gather(signal, 'vel', axis=0, tiled=True)]
    ppermute x0 -> x15, waiting for transfers between devices: none -> 13.1 us  [the longest x8 10.1 us: gather_around(): lower.append(lax.ppermute(lower[-1] if lower else array, axis, pairs))]
    gather x0 -> x2, local copies, waits for them, and re-layouts: none -> 8.1 us  [gather_around(): blocks = blocks[(jnp.arange(size) - shift) % size]]
    another operation x2 -> x1, local copies, waits for them, and re-layouts: 15 us -> 7.56 us  [widen(): images = jnp.stack([signal_part, weight_part], axis=1)]
    all_gather x1, blocking collectives: 23.7 us -> 18.6 us  [body(): lax.all_gather(weight, 'vel', axis=0, tiled=True)]
    pmax x1, blocking collectives: 59.1 us -> 61.9 us  [body(): best_likelihood = lax.pmax(jnp.max(likelihood, axis=0), 'vel')]
  transfers between devices with their start and end apart: 0 -> 15, of which waited for: 0 -> 11; matrix products, arithmetic and copies ran while one was open for 0% -> 5% of each run, Pallas kernels for 0% -> 0%
where the time goes in v1:
time: 199 us
  blocking collectives  80.5 us (40%)
  local copies, waits for them, and re-layouts  44 us (22%)
  other arithmetic  31.6 us (16%)
  starting transfers between devices  28.9 us (15%)
  waiting for transfers between devices  13.1 us (7%)
    pmax x1, blocking collectives, body(): best_likelihood = lax.pmax(jnp.max(likelihood, axis=0), 'vel')  61.9 us
    ppermute x7, starting transfers between devices, gather_around(): upper.append(lax.ppermute(upper[-1] if upper else array, axis, back))  28.4 us
    another operation x1, other arithmetic, widen(): images = jnp.stack([signal_part, weight_part], axis=1)  28.2 us
    gather x2, local copies, waits for them, and re-layouts, place_pair(): lax.dynamic_slice(padded, (anchor, anchor, col_start), (2, height, column...  24.4 us
    all_gather x1, blocking collectives, body(): lax.all_gather(weight, 'vel', axis=0, tiled=True)  18.6 us
    ppermute x8, waiting for transfers between devices, gather_around(): lower.append(lax.ppermute(lower[-1] if lower else array, axis, pairs))  10.1 us
    gather x2, local copies, waits for them, and re-layouts, gather_around(): blocks = blocks[(jnp.arange(size) - shift) % size]  8.1 us
    another operation x1, local copies, waits for them, and re-layouts, widen(): images = jnp.stack([signal_part, weight_part], axis=1)  7.56 us
  transfers between devices with their start and end apart: 15, of which 11 were waited for; matrix products, arithmetic and copies ran while one was open for 5% of the time, Pallas kernels for 0%

profile of v1, /device:TPU:0, one launch (start us, length us, event | category | flops | bytes accessed | tf_op | source)
XLA Modules:
  0.0 199.0 jit_solution(17865814947957237593)
XLA Ops:
  0.6 0.5 collective-permute-start
  1.2 5.0 %collective-permute-start.8 = (bf16[1,8,512]{2,1,0:T(8,128)(2,1)}, bf16[1,8,512]{2,1,0:T(8,128)(2,1)S(1)}, u32[]{:S(2)}, u32[]{:S(2)}) collective-permute-start(bf16[1,8,512]{2,1,0:T(8,128)(2,1)} %param.5), channel_id=1, source_target_pairs={{1,0},{2,1},{3,2},{4,3},{5,4},{6,5},{7,6},{8,7},{9,8},{10,9},{11,1... | collective-permute-start | bytes 24584 | tf_op jit(solution)/shard_map/ppermute | solution.py:22
  6.2 0.8 slice_bitcast_fusion.11
  7.0 0.2 fusion.58
  7.2 0.1 broadcast_divide_fusion
  7.3 0.1 copy.60
  7.4 0.3 collective-permute-done
  7.7 0.0 collective-permute-start.1
  7.7 0.1 multiply_reduce_fusion.1
  7.8 5.8 %collective-permute-done.1 = bf16[1,8,512]{2,1,0:T(8,128)(2,1)S(1)} collective-permute-done((bf16[1,8,512]{2,1,0:T(8,128)(2,1)S(1)}, bf16[1,8,512]{2,1,0:T(8,128)(2,1)S(1)}, u32[]{:S(2)}, u32[]{:S(2)}) %collective-permute-start.1) | collective-permute-done | bytes 8224 | tf_op jit(solution)/shard_map/ppermute | solution.py:20
  13.6 0.0 collective-permute-start.2
  13.6 0.0 collective-permute-done.8
  13.6 4.5 %collective-permute-start.9 = (bf16[1,8,512]{2,1,0:T(8,128)(2,1)S(1)}, bf16[1,8,512]{2,1,0:T(8,128)(2,1)S(1)}, u32[]{:S(2)}, u32[]{:S(2)}) collective-permute-start(bf16[1,8,512]{2,1,0:T(8,128)(2,1)S(1)} %collective-permute-done.8), channel_id=1, source_target_pairs={{1,0},{2,1},{3,2},{4,3},{5,4},{6,5},{7,6},{8,7},{9,8},{10,9},{11,1... | collective-permute-start | bytes 24584 | tf_op jit(solution)/shard_map/ppermute | solution.py:22
  18.1 1.3 collective-permute-done.2
  19.3 0.0 collective-permute-start.3
  19.4 0.1 collective-permute-done.9
  19.4 4.4 %collective-permute-start.10 = (bf16[1,8,512]{2,1,0:T(8,128)(2,1)S(1)}, bf16[1,8,512]{2,1,0:T(8,128)(2,1)S(1)}, u32[]{:S(2)}, u32[]{:S(2)}) collective-permute-start(bf16[1,8,512]{2,1,0:T(8,128)(2,1)S(1)} %collective-permute-done.9), channel_id=1, source_target_pairs={{1,0},{2,1},{3,2},{4,3},{5,4},{6,5},{7,6},{8,7},{9,8},{10,9},{11,1... | collective-permute-start | bytes 24584 | tf_op jit(solution)/shard_map/ppermute | solution.py:22
  23.9 1.3 collective-permute-done.3
  25.1 0.0 collective-permute-start.4
  25.1 0.8 or_bitcast_fusion
  25.9 4.5 %collective-permute-start.11 = (bf16[1,8,512]{2,1,0:T(8,128)(2,1)S(1)}, bf16[1,8,512]{2,1,0:T(8,128)(2,1)S(1)}, u32[]{:S(2)}, u32[]{:S(2)}) collective-permute-start(bf16[1,8,512]{2,1,0:T(8,128)(2,1)S(1)} %collective-permute-done.10), channel_id=1, source_target_pairs={{1,0},{2,1},{3,2},{4,3},{5,4},{6,5},{7,6},{8,7},{9,8},{10,9},{11,1... | collective-permute-start | bytes 24584 | tf_op jit(solution)/shard_map/ppermute | solution.py:22
  30.4 0.5 collective-permute-done.4
  30.9 0.9 collective-permute-done.11
  31.8 4.4 %collective-permute-start.12 = (bf16[1,8,512]{2,1,0:T(8,128)(2,1)S(1)}, bf16[1,8,512]{2,1,0:T(8,128)(2,1)S(1)}, u32[]{:S(2)}, u32[]{:S(2)}) collective-permute-start(bf16[1,8,512]{2,1,0:T(8,128)(2,1)S(1)} %collective-permute-done.11), channel_id=1, source_target_pairs={{1,0},{2,1},{3,2},{4,3},{5,4},{6,5},{7,6},{8,7},{9,8},{10,9},{11,1... | collective-permute-start | bytes 24584 | tf_op jit(solution)/shard_map/ppermute | solution.py:22
  36.2 0.5 collective-permute-done.5
  36.7 0.9 collective-permute-done.12
  37.5 4.4 %collective-permute-start.13 = (bf16[1,8,512]{2,1,0:T(8,128)(2,1)S(1)}, bf16[1,8,512]{2,1,0:T(8,128)(2,1)S(1)}, u32[]{:S(2)}, u32[]{:S(2)}) collective-permute-start(bf16[1,8,512]{2,1,0:T(8,128)(2,1)S(1)} %collective-permute-done.12), channel_id=1, source_target_pairs={{1,0},{2,1},{3,2},{4,3},{5,4},{6,5},{7,6},{8,7},{9,8},{10,9},{11,1... | collective-permute-start | bytes 24584 | tf_op jit(solution)/shard_map/ppermute | solution.py:22
  41.9 0.5 collective-permute-done.6
  42.4 0.0 collective-permute-start.7
  42.4 18.6 %all_gather.3 = bf16[16,8,512]{2,1,0:T(8,128)(2,1)S(1)} all-gather(bf16[1,8,512]{2,1,0:T(8,128)(2,1)} %param.6), channel_id=1, replica_groups=mesh['groups'=2,'vel'=16] {'vel'}, dimensions={0}, use_global_device_ids=true | all-gather | bytes 139264 | tf_op jit(solution)/shard_map/all_gather | solution.py:120
  61.0 7.6 %copy.75 = bf16[16,1,8,512]{2,1,0,3:T(2,128)(2,1)} copy(bf16[16,1,8,512]{3,2,0,1:T(8,128)(2,1)S(1)} %bitcast.104) | data formatting | bytes 262144 | tf_op jit(solution)/shard_map/stack | solution.py:109
  68.6 0.0 collective-permute-done.13
  68.6 1.1 collective-permute-start.14
  69.7 0.0 collective-permute-done.7
  69.9 1.2 collective-permute-done.14
  71.1 0.6 gather_fusion
  71.7 7.5 %copy.74 = bf16[16,1,8,512]{2,1,0,3:T(2,128)(2,1)} copy(bf16[16,1,8,512]{3,2,0,1:T(8,128)(2,1)S(1)} %bitcast.103) | data formatting | bytes 262144 | tf_op jit(solution)/shard_map/gather | solution.py:25
  79.2 28.2 %select_maximum_fusion = bf16[16,2,8,550]{2,1,0,3:T(2,128)(2,1)} fusion(bf16[16,1,8,512]{2,1,0,3:T(2,128)(2,1)} %copy.75, bf16[16,1,8,512]{2,1,0,3:T(2,128)(2,1)} %copy.74), kind=kLoop, calls=%fused_computation.4 | loop fusion | flops 1267200 | bytes 543744 | tf_op jit(solution)/shard_map/stack | solution.py:109
  107.4 15.2 %gather_fusion.1 = bf16[16,2,8,517]{2,1,3,0:T(2,128)(2,1)} fusion(bf16[16,2,8,550]{2,1,0,3:T(2,128)(2,1)} %select_maximum_fusion, s32[16]{0:T(128)S(1)} %get-tuple-element.42), kind=kCustom, calls=%fused_computation.1 | custom fusion | bytes 529664 | tf_op jit(solution)/shard_map/while/body/eval_jaxpr/vmap()/gather | solution.py:48
  122.6 9.2 %copy.76 = bf16[16,2,8,517]{3,2,1,0:T(8,128)(2,1)S(1)} copy(bf16[16,2,8,517]{2,1,3,0:T(2,128)(2,1)} %gather_fusion.1) | data formatting | bytes 529408 | tf_op jit(solution)/shard_map/while/body/eval_jaxpr/vmap()/gather | solution.py:48
  131.8 0.1 convert_element_type.40
  131.9 0.9 fusion.5
  132.8 0.4 copy.80
  133.2 0.5 pad.11.clone
  133.7 1.5 gather_fusion.2
  135.2 1.2 fusion.10
  136.5 61.9 %pmax.7 = f32[8,512]{1,0:T(8,128)} all-reduce(f32[8,512]{1,0:T(8,128)S(1)} %bitcast.108), channel_id=1, replica_groups=mesh['groups'=2,'vel'=16] {'vel'}, use_global_device_ids=true, to_apply=%region_4.6 | all-reduce | flops 4096 | bytes 32768 | tf_op jit(solution)/shard_map/pmax | solution.py:132
  198.4 0.6 copy.78
  (31 shorter events, 0.2 us)
Async XLA Ops:
  0.6 69.2 %copy-start = (bf16[1,8,512]{2,1,0:T(8,128)(2,1)S(1)}, bf16[1,8,512]{2,1,0:T(8,128)(2,1)}, u32[]{:S(2)}) copy-start(bf16[1,8,512]{2,1,0:T(8,128)(2,1)} %param.5) | copy-start | bytes 24580
  0.6 7.1 %collective-permute-start = (bf16[1,8,512]{2,1,0:T(8,128)(2,1)}, bf16[1,8,512]{2,1,0:T(8,128)(2,1)S(1)}, u32[]{:S(2)}, u32[]{:S(2)}) collective-permute-start(bf16[1,8,512]{2,1,0:T(8,128)(2,1)} %param.5), channel_id=1, source_target_pairs={{0,1},{1,2},{2,3},{3,4},{4,5},{5,6},{6,7},{7,8},{8,9},{9,10},{10,1... | collective-permute-start | bytes 24584 | tf_op jit(solution)/shard_map/ppermute | solution.py:20
  1.2 12.4 %collective-permute-start.8 = (bf16[1,8,512]{2,1,0:T(8,128)(2,1)}, bf16[1,8,512]{2,1,0:T(8,128)(2,1)S(1)}, u32[]{:S(2)}, u32[]{:S(2)}) collective-permute-start(bf16[1,8,512]{2,1,0:T(8,128)(2,1)} %param.5), channel_id=1, source_target_pairs={{1,0},{2,1},{3,2},{4,3},{5,4},{6,5},{7,6},{8,7},{9,8},{10,9},{11,1... | collective-permute-start | bytes 24584 | tf_op jit(solution)/shard_map/ppermute | solution.py:22
  7.7 5.9 %collective-permute-start.1 = (bf16[1,8,512]{2,1,0:T(8,128)(2,1)S(1)}, bf16[1,8,512]{2,1,0:T(8,128)(2,1)S(1)}, u32[]{:S(2)}, u32[]{:S(2)}) collective-permute-start(bf16[1,8,512]{2,1,0:T(8,128)(2,1)S(1)} %collective-permute-done), channel_id=1, source_target_pairs={{0,1},{1,2},{2,3},{3,4},{4,5},{5,6},{6,7},{7,8},{8,9},{9,10},{10,1... | collective-permute-start | bytes 24584 | tf_op jit(solution)/shard_map/ppermute | solution.py:20
  13.6 5.8 %collective-permute-start.2 = (bf16[1,8,512]{2,1,0:T(8,128)(2,1)S(1)}, bf16[1,8,512]{2,1,0:T(8,128)(2,1)S(1)}, u32[]{:S(2)}, u32[]{:S(2)}) collective-permute-start(bf16[1,8,512]{2,1,0:T(8,128)(2,1)S(1)} %collective-permute-done.1), channel_id=1, source_target_pairs={{0,1},{1,2},{2,3},{3,4},{4,5},{5,6},{6,7},{7,8},{8,9},{9,10},{10,1... | collective-permute-start | bytes 24584 | tf_op jit(solution)/shard_map/ppermute | solution.py:20
  13.6 5.9 %collective-permute-start.9 = (bf16[1,8,512]{2,1,0:T(8,128)(2,1)S(1)}, bf16[1,8,512]{2,1,0:T(8,128)(2,1)S(1)}, u32[]{:S(2)}, u32[]{:S(2)}) collective-permute-start(bf16[1,8,512]{2,1,0:T(8,128)(2,1)S(1)} %collective-permute-done.8), channel_id=1, source_target_pairs={{1,0},{2,1},{3,2},{4,3},{5,4},{6,5},{7,6},{8,7},{9,8},{10,9},{11,1... | collective-permute-start | bytes 24584 | tf_op jit(solution)/shard_map/ppermute | solution.py:22
  19.3 5.8 %collective-permute-start.3 = (bf16[1,8,512]{2,1,0:T(8,128)(2,1)S(1)}, bf16[1,8,512]{2,1,0:T(8,128)(2,1)S(1)}, u32[]{:S(2)}, u32[]{:S(2)}) collective-permute-start(bf16[1,8,512]{2,1,0:T(8,128)(2,1)S(1)} %collective-permute-done.2), channel_id=1, source_target_pairs={{0,1},{1,2},{2,3},{3,4},{4,5},{5,6},{6,7},{7,8},{8,9},{9,10},{10,1... | collective-permute-start | bytes 24584 | tf_op jit(solution)/shard_map/ppermute | solution.py:20
  19.4 6.4 %collective-permute-start.10 = (bf16[1,8,512]{2,1,0:T(8,128)(2,1)S(1)}, bf16[1,8,512]{2,1,0:T(8,128)(2,1)S(1)}, u32[]{:S(2)}, u32[]{:S(2)}) collective-permute-start(bf16[1,8,512]{2,1,0:T(8,128)(2,1)S(1)} %collective-permute-done.9), channel_id=1, source_target_pairs={{1,0},{2,1},{3,2},{4,3},{5,4},{6,5},{7,6},{8,7},{9,8},{10,9},{11,1... | collective-permute-start | bytes 24584 | tf_op jit(solution)/shard_map/ppermute | solution.py:22
  25.1 5.8 %collective-permute-start.4 = (bf16[1,8,512]{2,1,0:T(8,128)(2,1)S(1)}, bf16[1,8,512]{2,1,0:T(8,128)(2,1)S(1)}, u32[]{:S(2)}, u32[]{:S(2)}) collective-permute-start(bf16[1,8,512]{2,1,0:T(8,128)(2,1)S(1)} %collective-permute-done.3), channel_id=1, source_target_pairs={{0,1},{1,2},{2,3},{3,4},{4,5},{5,6},{6,7},{7,8},{8,9},{9,10},{10,1... | collective-permute-start | bytes 24584 | tf_op jit(solution)/shard_map/ppermute | solution.py:20
  25.9 5.9 %collective-permute-start.11 = (bf16[1,8,512]{2,1,0:T(8,128)(2,1)S(1)}, bf16[1,8,512]{2,1,0:T(8,128)(2,1)S(1)}, u32[]{:S(2)}, u32[]{:S(2)}) collective-permute-start(bf16[1,8,512]{2,1,0:T(8,128)(2,1)S(1)} %collective-permute-done.10), channel_id=1, source_target_pairs={{1,0},{2,1},{3,2},{4,3},{5,4},{6,5},{7,6},{8,7},{9,8},{10,9},{11,1... | collective-permute-start | bytes 24584 | tf_op jit(solution)/shard_map/ppermute | solution.py:22
  30.9 5.8 %collective-permute-start.5 = (bf16[1,8,512]{2,1,0:T(8,128)(2,1)S(1)}, bf16[1,8,512]{2,1,0:T(8,128)(2,1)S(1)}, u32[]{:S(2)}, u32[]{:S(2)}) collective-permute-start(bf16[1,8,512]{2,1,0:T(8,128)(2,1)S(1)} %collective-permute-done.4), channel_id=1, source_target_pairs={{0,1},{1,2},{2,3},{3,4},{4,5},{5,6},{6,7},{7,8},{8,9},{9,10},{10,1... | collective-permute-start | bytes 24584 | tf_op jit(solution)/shard_map/ppermute | solution.py:20
  31.8 5.8 %collective-permute-start.12 = (bf16[1,8,512]{2,1,0:T(8,128)(2,1)S(1)}, bf16[1,8,512]{2,1,0:T(8,128)(2,1)S(1)}, u32[]{:S(2)}, u32[]{:S(2)}) collective-permute-start(bf16[1,8,512]{2,1,0:T(8,128)(2,1)S(1)} %collective-permute-done.11), channel_id=1, source_target_pairs={{1,0},{2,1},{3,2},{4,3},{5,4},{6,5},{7,6},{8,7},{9,8},{10,9},{11,1... | collective-permute-start | bytes 24584 | tf_op jit(solution)/shard_map/ppermute | solution.py:22
  36.7 5.8 %collective-permute-start.6 = (bf16[1,8,512]{2,1,0:T(8,128)(2,1)S(1)}, bf16[1,8,512]{2,1,0:T(8,128)(2,1)S(1)}, u32[]{:S(2)}, u32[]{:S(2)}) collective-permute-start(bf16[1,8,512]{2,1,0:T(8,128)(2,1)S(1)} %collective-permute-done.5), channel_id=1, source_target_pairs={{0,1},{1,2},{2,3},{3,4},{4,5},{5,6},{6,7},{7,8},{8,9},{9,10},{10,1... | collective-permute-start | bytes 24584 | tf_op jit(solution)/shard_map/ppermute | solution.py:20
  37.5 31.0 %collective-permute-start.13 = (bf16[1,8,512]{2,1,0:T(8,128)(2,1)S(1)}, bf16[1,8,512]{2,1,0:T(8,128)(2,1)S(1)}, u32[]{:S(2)}, u32[]{:S(2)}) collective-permute-start(bf16[1,8,512]{2,1,0:T(8,128)(2,1)S(1)} %collective-permute-done.12), channel_id=1, source_target_pairs={{1,0},{2,1},{3,2},{4,3},{5,4},{6,5},{7,6},{8,7},{9,8},{10,9},{11,1... | collective-permute-start | bytes 24584 | tf_op jit(solution)/shard_map/ppermute | solution.py:22
  42.4 27.3 %collective-permute-start.7 = (bf16[1,8,512]{2,1,0:T(8,128)(2,1)S(1)}, bf16[1,8,512]{2,1,0:T(8,128)(2,1)S(1)}, u32[]{:S(2)}, u32[]{:S(2)}) collective-permute-start(bf16[1,8,512]{2,1,0:T(8,128)(2,1)S(1)} %collective-permute-done.6), channel_id=1, source_target_pairs={{0,1},{1,2},{2,3},{3,4},{4,5},{5,6},{6,7},{7,8},{8,9},{9,10},{10,1... | collective-permute-start | bytes 24584 | tf_op jit(solution)/shard_map/ppermute | solution.py:20
  68.6 2.5 %collective-permute-start.14 = (bf16[1,8,512]{2,1,0:T(8,128)(2,1)S(1)}, bf16[1,8,512]{2,1,0:T(8,128)(2,1)S(1)}, u32[]{:S(2)}, u32[]{:S(2)}) collective-permute-start(bf16[1,8,512]{2,1,0:T(8,128)(2,1)S(1)} %collective-permute-done.13), channel_id=1, source_target_pairs={{1,0},{2,1},{3,2},{4,3},{5,4},{6,5},{7,6},{8,7},{9,8},{10,9},{11,1... | collective-permute-start | bytes 24584 | tf_op jit(solution)/shard_map/ppermute | solution.py:22
